TPU v7x, 32 devices: a whole 2x2x4 slice. The times are simulated.
32 devices in a mesh: inst: 4 (over x, core), space: 8 (over z, y).
Axes of the slice: x: 2, y: 2, z: 4, core: 2. Of those that a mesh axis runs over, the one named last changes fastest.
Arguments:
- adjoint_old: float32 [8, 6, 512, 512], P('inst', None, 'space'), may hold values from -6 to 6
- source_term: float32 [8, 6, 512, 512], P('inst', None, 'space'), may hold values from -6 to 6
- face_stream: float32 [8, 512, 512], P('inst', 'space'), may hold values from 0.2 to 1
- face_pitch: float32 [8, 512, 512], P('inst', 'space'), may hold values from 0.2 to 1
- diag_scale: float32 [8, 512, 512], P('inst', 'space'), may hold values from 0.1 to 0.4
- volume: float32 [512, 512], P('space'), may hold values from 0.5 to 2
- face_blocks: float32 [4, 6, 6], replicated, may hold values from -2.5 to 2.5
- diag_inverse: float32 [8, 6, 6], P('inst')
- periodic_block: float32 [6, 6], replicated, may hold values from -2.5 to 2.5
- frequency: float32 [1], replicated, may hold values from 0.5 to 2
- phase_shift: int32 [1], replicated, may hold values from 1 to 7
- periodic_cells: int32 [8, 8, 128], P('space'), may hold values from 0 to 32767
- periodic_targets: int32 [8, 8, 128], P(None, 'space'), may hold values from 0 to 32767
- periodic_weights: float32 [8, 8, 128], P('space'), may hold values from 0.5 to 1.5
- periodic_counts: int32 [8, 8], P('space'), may hold values from 0 to 128, as said below
Outputs:
- adjoint_new: float32 [8, 6, 512, 512], P('inst', None, 'space')
- residual: float32 [8, 6, 512, 512], P('inst', None, 'space')
Inputs may be any that keep to these rules, and one draw needn't show every extreme that they name: `periodic_counts`: each partition's row has one peer with 128 live faces, and one partition receives 128 live faces from every partition. `periodic_cells`: local cell indices in the sending partition. `periodic_targets`: local cell indices in the receiving partition.
All inputs are finite; a program needn't handle non-finite values.
Results may differ from a plain program's by a relative error of at most 0.0001.
Values sent between devices are 32-bit elements; how exact they have to be, the bound alone decides.
A program may use at most 128 MiB of HBM per device.

v0:
```python
import functools
import math

import jax
import jax.numpy as jnp
from jax import lax
from jax.experimental import pallas as pl
from jax.experimental.pallas import tpu as pltpu
from jax.sharding import PartitionSpec as P

SWEEPS = 2
TILE = 8
LANES = 128
WINDOW = 4
MESH = pl.DeviceIdType.MESH


def spectral_entry(offset, count):
    offset = offset % count
    if offset == 0 or 2 * offset == count:
        return 0.0
    return 0.5 * (-1.0) ** offset / math.tan(math.pi * offset / count)


def split_parts(value):
    parts = []
    for _ in range(3):
        part = value.astype(jnp.bfloat16)
        parts.append(part)
        value = value - part.astype(jnp.float32)
    return parts


def kernel(
    n_space,
    a_hbm,
    s_hbm,
    fs_hbm,
    fp_hbm,
    ds_hbm,
    vol_hbm,
    blocks,
    dinv,
    pblock,
    freq,
    shift,
    cells,
    targets,
    weights,
    counts,
    out_a,
    out_r,
    A,
    SP,
    R,
    FS,
    FP,
    DS,
    VOL,
    RX,
    SB,
    RL,
    COL,
    PICK,
    ALLP,
    ROUTED,
    ARR,
    load_sem,
    xs,
    xr,
    rs,
    rr,
    ss,
    sr,
    hs,
    hr,
    ps,
    pr,
    as_,
    ar,
    oa,
    orr,
):
    per_dev, variables, rows, width = a_hbm.shape
    instances = 4 * per_dev
    slots = cells.shape[2]
    nb = rows // TILE
    total = SWEEPS * nb
    inst = lax.axis_index("inst")
    me = lax.axis_index("space")
    odd = inst % 2
    sibling = inst + 1 - 2 * odd
    across = (inst + 2) % 4
    shift_bits = width.bit_length() - 1

    def local(src, dst, n):
        return pltpu.make_async_copy(src, dst, load_sem.at[n])

    inner = pl.ds(TILE, rows)
    loads = [
        local(a_hbm, A.at[0, :, :, inner, :], 0),
        local(fs_hbm, FS.at[:, inner, :], 1),
        local(s_hbm, SP, 2),
        local(fp_hbm, FP, 3),
        local(ds_hbm, DS, 4),
        local(vol_hbm, VOL, 5),
    ]
    for copy in loads:
        copy.start()

    barrier = pltpu.get_barrier_semaphore()
    pl.semaphore_signal(barrier, inc=1, device_id={"inst": sibling}, device_id_type=MESH)
    pl.semaphore_signal(barrier, inc=1, device_id={"inst": across}, device_id_type=MESH)

    @pl.loop(1, n_space)
    def _(j):
        pl.semaphore_signal(
            barrier, inc=1, device_id={"space": (me + j) % n_space}, device_id_type=MESH
        )

    def remote(src, dst, send, recv, **device):
        return pltpu.make_async_remote_copy(
            src_ref=src, dst_ref=dst, send_sem=send, recv_sem=recv, device_id=device,
            device_id_type=MESH,
        )

    def place(t):
        sweep = t // nb
        block = (t % nb + nb - 1) % nb
        return sweep, block, pl.multiple_of(block * TILE, TILE)

    def x_copy(t):
        sweep, _, row = place(t)
        return remote(
            A.at[sweep, :, :, pl.ds(row + TILE, TILE), :],
            RX.at[sweep, :, :, pl.ds(row, TILE), :],
            xs.at[t], xr.at[t], inst=across,
        )

    def sib_copy(t):
        sweep, _, row = place(t)
        return remote(
            A.at[sweep, :, :, pl.ds(row + TILE, TILE), :],
            SB.at[sweep, :, :, pl.ds(row, TILE), :],
            ss.at[t], sr.at[t], inst=sibling,
        )

    def relay_copy(t):
        sweep, _, row = place(t)
        here = RX.at[sweep, :, :, pl.ds(row, TILE), :]
        return remote(
            here, RL.at[sweep, :, :, pl.ds(row, TILE), :], rs.at[t], rr.at[t], inst=sibling
        )

    has_above = me < n_space - 1
    has_below = me > 0
    above = (me + 1) % n_space
    below = (me + n_space - 1) % n_space

    def halo_up(sweep):
        return remote(
            A.at[sweep, :, :, pl.ds(rows, TILE), :],
            A.at[sweep, :, :, pl.ds(0, TILE), :],
            hs.at[2 * sweep], hr.at[2 * sweep], space=above,
        )

    def halo_down(sweep):
        return remote(
            A.at[sweep, :, :, pl.ds(TILE, TILE), :],
            A.at[sweep, :, :, pl.ds(rows + TILE, TILE), :],
            hs.at[2 * sweep + 1], hr.at[2 * sweep + 1], space=below,
        )

    def halo_face():
        last = 2 * SWEEPS
        return remote(
            FS.at[:, pl.ds(rows, TILE), :], FS.at[:, pl.ds(0, TILE), :],
            hs.at[last], hr.at[last], space=above,
        )

    @pl.when(me == 0)
    def _():
        FS[:, 0:TILE, :] = jnp.zeros((per_dev, TILE, width), jnp.float32)
        for sweep in range(SWEEPS):
            A[sweep, :, :, 0:TILE, :] = jnp.zeros((per_dev, variables, TILE, width), jnp.float32)

    @pl.when(me == n_space - 1)
    def _():
        for sweep in range(SWEEPS):
            A[sweep, :, :, rows + TILE : rows + 2 * TILE, :] = jnp.zeros(
                (per_dev, variables, TILE, width), jnp.float32
            )

    loads[0].wait()
    pl.semaphore_wait(barrier, n_space + 1)
    for t in range(WINDOW):
        x_copy(t).start()
    loads[1].wait()

    @pl.when(has_above)
    def _():
        halo_up(0).start()
        halo_face().start()

    @pl.when(has_below)
    def _():
        halo_down(0).start()

    @pl.loop(0, nb)
    def _(t):
        sib_copy(t).start()

    sub_w = lax.broadcasted_iota(jnp.int32, (width, slots), 0)
    sub_r = lax.broadcasted_iota(jnp.int32, (rows, slots), 0)

    def column_table(index, chunk):
        for q in range(TILE):
            line = index(chunk * TILE + q)
            column = jnp.bitwise_and(line, width - 1)
            hot = jnp.where(sub_w == column, 1.0, 0.0).astype(jnp.bfloat16)
            COL[:, q * slots : (q + 1) * slots] = hot

    def cell_line(q):
        return cells[0, pl.ds(q, 1), :]

    def target_line(p):
        return targets[p, 0:1, :]

    chunks = n_space // TILE

    @pl.loop(0, chunks)
    def _(chunk):
        column_table(cell_line, chunk)

        @pl.loop(0, per_dev)
        def _(k):
            field = A[0, k, :, TILE : TILE + rows, :].reshape(variables * rows, width)
            found = None
            for part in split_parts(field):
                term = jnp.dot(part, COL[...], preferred_element_type=jnp.float32)
                found = term if found is None else found + term
            for q in range(TILE):
                hit = sub_r == lax.shift_right_logical(cell_line(chunk * TILE + q), shift_bits)
                for v in range(variables):
                    piece = found[v * rows : (v + 1) * rows, q * slots : (q + 1) * slots]
                    PICK[k, v, chunk, q : q + 1, :] = jnp.sum(
                        jnp.where(hit, piece, 0.0), axis=0, keepdims=True
                    )

        lane = lax.broadcasted_iota(jnp.int32, (TILE, slots), 1)
        sub = lax.broadcasted_iota(jnp.int32, (TILE, slots), 0)
        limit = jnp.zeros((TILE, slots), jnp.int32)
        for q in range(TILE):
            limit = jnp.where(sub == q, counts[0, chunk * TILE + q], limit)
        first = pl.multiple_of(chunk * TILE, TILE)
        weight = jnp.where(lane < limit, weights[0, pl.ds(first, TILE), :], 0.0)

        for k in range(per_dev):
            picked = [PICK[k, v, chunk] for v in range(variables)]
            for u in range(variables):
                mixed = pblock[0, u] * picked[0]
                for v in range(1, variables):
                    mixed = mixed + pblock[v, u] * picked[v]
                ALLP[0, k, u, chunk] = mixed * weight

    p_x = remote(ALLP.at[0], ALLP.at[2], ps.at[0], pr.at[0], inst=across)
    p_sib = remote(ALLP.at[0], ALLP.at[3 - 2 * odd], ps.at[1], pr.at[1 + odd], inst=sibling)
    p_rel = remote(ALLP.at[2], ALLP.at[1 + 2 * odd], ps.at[2], pr.at[2 - odd], inst=sibling)
    p_sib_in = remote(ALLP.at[0], ALLP.at[1 + 2 * odd], ps.at[1], pr.at[2 - odd], inst=sibling)
    p_rel_in = remote(ALLP.at[2], ALLP.at[3 - 2 * odd], ps.at[2], pr.at[1 + odd], inst=sibling)
    p_x.start()
    p_sib.start()
    p_x.wait_recv()
    p_rel.start()
    p_sib_in.wait_recv()
    p_rel_in.wait_recv()
    for k in range(per_dev):
        wanted = lax.rem(k - shift[0] + 2 * instances, instances)
        group = lax.div(wanted, per_dev)
        member = lax.rem(wanted, per_dev)

        @pl.loop(0, chunks)
        def _(chunk):
            for u in range(variables):
                value = ALLP[group, member, u, chunk]
                for q in range(TILE):
                    ROUTED[chunk * TILE + q, k * variables + u : k * variables + u + 1, :] = value[
                        q : q + 1, :
                    ]

    def a2a(j):
        return remote(
            ROUTED.at[(me + j) % n_space], ARR.at[me], as_.at[j], ar.at[j],
            space=(me + j) % n_space,
        )

    @pl.loop(1, n_space)
    def _(j):
        a2a(j).start()

    ARR[me] = ROUTED[me]
    loads[2].wait()
    column_table(target_line, 0)

    @pl.loop(1, n_space)
    def _(j):
        remote(
            ROUTED.at[0], ARR.at[(me + n_space - j) % n_space], as_.at[j], ar.at[j],
            space=(me + j) % n_space,
        ).wait_recv()

    @pl.loop(0, chunks)
    def _(chunk):
        if chunks > 1:
            column_table(target_line, chunk)

        for k in range(per_dev):
            arrived = [
                split_parts(ARR[chunk * TILE + p, k * variables : (k + 1) * variables, :])
                for p in range(TILE)
            ]
            hits = [
                sub_r == lax.shift_right_logical(target_line(chunk * TILE + p), shift_bits)
                for p in range(TILE)
            ]
            for u in range(variables):
                total_u = None
                for part in range(3):
                    spread = jnp.concatenate(
                        [
                            jnp.where(
                                hits[p], arrived[p][part][u : u + 1, :].astype(jnp.float32), 0.0
                            ).astype(jnp.bfloat16)
                            for p in range(TILE)
                        ],
                        axis=1,
                    )
                    term = lax.dot_general(
                        spread, COL[...], (((1,), (1,)), ((), ())),
                        preferred_element_type=jnp.float32,
                    )
                    total_u = term if total_u is None else total_u + term
                SP[k, u] = SP[k, u] - total_u

    for copy in loads[3:]:
        copy.wait()

    @pl.when(has_below)
    def _():
        halo_up(0).wait_recv()
        halo_face().wait_recv()

    @pl.when(has_above)
    def _():
        halo_down(0).wait_recv()

    d1, d2, d3 = (spectral_entry(d, instances) for d in (1, 2, 3))
    is_odd = odd == 1

    def pick(even_value, odd_value):
        return jnp.where(is_odd, jnp.float32(odd_value), jnp.float32(even_value))

    nxt = ((d2, d3), (d1, d2))
    prv = ((-d2, -d1), (-d3, -d2))
    c_sib = [[pick(nxt[g][m], prv[g][m]) for m in range(2)] for g in range(2)]
    c_rel = [[pick(prv[g][m], nxt[g][m]) for m in range(2)] for g in range(2)]
    c_own = (d1, -d1)
    c_x = (-d3, d3)

    sub8 = lax.broadcasted_iota(jnp.int32, (TILE, width), 0)
    lane8 = lax.broadcasted_iota(jnp.int32, (TILE, width), 1)

    @pl.loop(0, total)
    def _(t):
        sweep, block, row = place(t)
        here = pl.ds(row, TILE)
        mid = pl.ds(row + TILE, TILE)
        low = pl.ds(row, TILE)
        high = pl.ds(row + 2 * TILE, TILE)

        x_copy(t).wait()

        @pl.when(t + WINDOW < total)
        def _():
            x_copy(t + WINDOW).start()

        relay_copy(t).start()

        @pl.when(t == nb)
        def _():
            @pl.when(has_below)
            def _():
                halo_up(1).wait_recv()

            @pl.when(has_above)
            def _():
                halo_down(1).wait_recv()

        sib_copy(t).wait_recv()
        relay_copy(t).wait_recv()
        scaled = freq[0] * VOL[here, :]

        for k in range(per_dev):
            other = 1 - k
            acc = []
            for u in range(variables):
                s = c_own[k] * A[sweep, other, u, mid, :] + c_x[k] * RX[sweep, other, u, here, :]
                for m in range(2):
                    s = s + c_sib[k][m] * SB[sweep, m, u, here, :]
                    s = s + c_rel[k][m] * RL[sweep, m, u, here, :]
                acc.append(SP[k, u, here, :] - scaled * s)
            fs_low = jnp.where(sub8 == TILE - 1, FS[k, low, :], FS[k, mid, :])
            fs_mid = FS[k, mid, :]
            fp = jnp.where(lane8 == width - 1, 0.0, FP[k, here, :])
            for v in range(variables):
                a = A[sweep, k, v, mid, :]
                x = pltpu.roll(
                    fs_low * jnp.where(sub8 == TILE - 1, A[sweep, k, v, low, :], a), 1, 0
                )
                y = fs_mid * pltpu.roll(
                    jnp.where(sub8 == 0, A[sweep, k, v, high, :], a), TILE - 1, 0
                )
                left = pltpu.roll(fp * a, 1, 1)
                right = fp * pltpu.roll(a, width - 1, 1)
                for u in range(variables):
                    acc[u] = acc[u] - (
                        (blocks[0, v, u] * x + blocks[1, v, u] * y)
                        + (blocks[2, v, u] * left + blocks[3, v, u] * right)
                    )
            scale = DS[k, here, :]
            for u in range(variables):
                R[k, u, here, :] = acc[u]
            for u in range(variables):
                new = dinv[k, u, 0] * acc[0]
                for v in range(1, variables):
                    new = new + dinv[k, u, v] * acc[v]
                A[sweep + 1, k, u, mid, :] = scale * new

        @pl.when(sweep == 0)
        def _():
            sib_copy(t + nb).start()

        @pl.when(t == 1)
        def _():
            @pl.when(has_above)
            def _():
                halo_up(1).start()

            @pl.when(has_below)
            def _():
                halo_down(1).start()

        @pl.when(sweep == SWEEPS - 1)
        def _():
            pltpu.make_async_copy(
                A.at[SWEEPS, :, :, mid, :], out_a.at[:, :, here, :], oa.at[block]
            ).start()
            pltpu.make_async_copy(
                R.at[:, :, here, :], out_r.at[:, :, here, :], orr.at[block]
            ).start()

    @pl.loop(0, total)
    def _(t):
        relay_copy(t).wait_send()
        sib_copy(t).wait_send()

    p_x.wait_send()
    p_sib.wait_send()
    p_rel.wait_send()

    @pl.loop(1, n_space)
    def _(j):
        a2a(j).wait_send()

    @pl.when(has_above)
    def _():
        for sweep in range(SWEEPS):
            halo_up(sweep).wait_send()
        halo_face().wait_send()

    @pl.when(has_below)
    def _():
        for sweep in range(SWEEPS):
            halo_down(sweep).wait_send()

    @pl.loop(0, nb)
    def _(b):
        here = pl.ds(pl.multiple_of(b * TILE, TILE), TILE)
        mid = pl.ds(pl.multiple_of(b * TILE, TILE) + TILE, TILE)
        pltpu.make_async_copy(
            A.at[SWEEPS, :, :, mid, :], out_a.at[:, :, here, :], oa.at[b]
        ).wait()
        pltpu.make_async_copy(R.at[:, :, here, :], out_r.at[:, :, here, :], orr.at[b]).wait()


def body(n_space, *args):
    per_dev, variables, rows, width = args[0].shape
    slots = args[11].shape[2]
    nb = rows // TILE
    chunks = n_space // TILE
    total = SWEEPS * nb
    f32 = jnp.float32
    hbm = pl.BlockSpec(memory_space=pl.ANY)
    smem = pl.BlockSpec(memory_space=pltpu.SMEM)
    vmem = pl.BlockSpec(memory_space=pltpu.VMEM)
    dma = pltpu.SemaphoreType.DMA
    field = (per_dev, variables, rows, width)
    out = jax.ShapeDtypeStruct(field, f32)
    return pl.pallas_call(
        functools.partial(kernel, n_space),
        out_shape=(out, out),
        in_specs=[hbm] * 6 + [smem] * 5 + [vmem] * 3 + [smem],
        out_specs=(hbm, hbm),
        scratch_shapes=[
            pltpu.VMEM((SWEEPS + 1, per_dev, variables, rows + 2 * TILE, width), f32),
            pltpu.VMEM(field, f32),
            pltpu.VMEM(field, f32),
            pltpu.VMEM((per_dev, rows + TILE, width), f32),
            pltpu.VMEM((per_dev, rows, width), f32),
            pltpu.VMEM((per_dev, rows, width), f32),
            pltpu.VMEM((rows, width), f32),
            pltpu.VMEM((SWEEPS,) + field, f32),
            pltpu.VMEM((SWEEPS,) + field, f32),
            pltpu.VMEM((SWEEPS,) + field, f32),
            pltpu.VMEM((width, TILE * slots), jnp.bfloat16),
            pltpu.VMEM((per_dev, variables, chunks, TILE, slots), f32),
            pltpu.VMEM((4, per_dev, variables, chunks, TILE, slots), f32),
            pltpu.VMEM((n_space, per_dev * variables, slots), f32),
            pltpu.VMEM((n_space, per_dev * variables, slots), f32),
            dma((6,)),
            dma((total,)),
            dma((total,)),
            dma((total,)),
            dma((total,)),
            dma((total,)),
            dma((total,)),
            dma((2 * SWEEPS + 1,)),
            dma((2 * SWEEPS + 1,)),
            dma((3,)),
            dma((3,)),
            dma((n_space,)),
            dma((n_space,)),
            dma((nb,)),
            dma((nb,)),
        ],
        compiler_params=pltpu.CompilerParams(
            collective_id=0, has_side_effects=True, vmem_limit_bytes=56 * 1024 * 1024
        ),
    )(*args)


def solution(mesh):
    in_specs = (
        P("inst", None, "space", None),
        P("inst", None, "space", None),
        P("inst", "space", None),
        P("inst", "space", None),
        P("inst", "space", None),
        P("space", None),
        P(),
        P("inst", None, None),
        P(),
        P(),
        P(),
        P("space", None, None),
        P(None, "space", None),
        P("space", None, None),
        P("space", None),
    )
    out_specs = (P("inst", None, "space", None), P("inst", None, "space", None))
    return jax.shard_map(
        functools.partial(body, mesh.shape["space"]),
        mesh=mesh,
        in_specs=in_specs,
        out_specs=out_specs,
        check_vma=False,
    )
```

profile of v0, /device:TPU:1, one launch (start us, length us, event | category | flops | bytes accessed | tf_op | source)
XLA Modules:
  0.0 106.5 jit_solution(12623500044606887098)
XLA Ops:
  1.9 1.3 %copy.18.dinv = f32[2,6,6]{2,1,0:T(8,128)} copy(f32[2,6,6]{2,0,1:T(2,128)} %param.22) | data formatting | bytes 576 | tf_op args[7]
  3.2 1.3 %copy.17.blocks = f32[4,6,6]{2,1,0:T(8,128)} copy(f32[4,6,6]{2,0,1:T(4,128)} %param.21) | data formatting | bytes 1152 | tf_op args[6]
  4.5 98.0 %shard_map.158 = (f32[2,6,64,512]{3,2,1,0:T(8,128)}, f32[2,6,64,512]{3,2,1,0:T(8,128)}) custom-call(f32[2,6,64,512]{3,2,1,0:T(8,128)} %a_hbm.1, f32[2,6,64,512]{3,2,1,0:T(8,128)} %s_hbm.1, f32[2,64,512]{2,1,0:T(8,128)} %fs_hbm.1, f32[2,64,512]{2,1,0:T(8,128)} %fp_hbm.1, f32[2,64,512]{2,1,0:T(8,128)} %ds_hbm.1, f32[64,512]{1,0:T(8,128)} %vol_hbm.1, ...), custom_call_target="tpu_custom_call" | custom-call | tf_op jit(solution)/shard_map/pallas_call | solution.py:509
  102.6 0.0 copy-start
  102.6 2.8 %copy.23 = f32[2,6,64,512]{3,2,1,0:T(8,128)} copy(f32[2,6,64,512]{3,2,1,0:T(8,128)} %get-tuple-element.4) | data formatting | bytes 3145728
  105.3 0.0 copy-done
  105.4 1.1 %copy.24 = f32[2,6,64,512]{3,2,1,0:T(8,128)} copy(f32[2,6,64,512]{3,2,1,0:T(8,128)S(1)} %copy-done) | data formatting | bytes 3145728
Async XLA Ops:
  102.6 2.8 %copy-start = (f32[2,6,64,512]{3,2,1,0:T(8,128)S(1)}, f32[2,6,64,512]{3,2,1,0:T(8,128)}, u32[]{:S(2)}) copy-start(f32[2,6,64,512]{3,2,1,0:T(8,128)} %get-tuple-element.5) | copy-start | bytes 4718596
where the time goes:
time: 107 us; the launch traced here: 106 us
  Pallas kernels  98 us (92%)
  local copies, waits for them, and re-layouts  6.54 us (6%)
  between operations  1.94 us (2%)
    pallas_call x1, Pallas kernels, body(): pl.pallas_call(functools.partial(kernel, n_space), out_shape=(out, out),...  98 us
    unnamed x6, local copies, waits for them, and re-layouts  6.54 us

commit v1 on v0

--- a/solution.py
+++ b/solution.py
@@ -11,7 +11,8 @@
 SWEEPS = 2
 TILE = 8
 LANES = 128
-WINDOW = 4
+WINDOW = 3
+PARTS = 2
 MESH = pl.DeviceIdType.MESH
 
 
@@ -24,7 +25,7 @@
 
 def split_parts(value):
     parts = []
-    for _ in range(3):
+    for _ in range(PARTS):
         part = value.astype(jnp.bfloat16)
         parts.append(part)
         value = value - part.astype(jnp.float32)
@@ -65,6 +66,7 @@
     ALLP,
     ROUTED,
     ARR,
+    LHS,
     load_sem,
     xs,
     xr,
@@ -152,6 +154,10 @@
             here, RL.at[sweep, :, :, pl.ds(row, TILE), :], rs.at[t], rr.at[t], inst=sibling
         )
 
+    def forward(t):
+        x_copy(t).wait()
+        relay_copy(t).start()
+
     has_above = me < n_space - 1
     has_below = me > 0
     above = (me + 1) % n_space
@@ -193,8 +199,11 @@
 
     loads[0].wait()
     pl.semaphore_wait(barrier, n_space + 1)
-    for t in range(WINDOW):
+
+    @pl.loop(0, nb)
+    def _(t):
         x_copy(t).start()
+
     loads[1].wait()
 
     @pl.when(has_above)
@@ -235,10 +244,12 @@
         @pl.loop(0, per_dev)
         def _(k):
             field = A[0, k, :, TILE : TILE + rows, :].reshape(variables * rows, width)
-            found = None
-            for part in split_parts(field):
-                term = jnp.dot(part, COL[...], preferred_element_type=jnp.float32)
-                found = term if found is None else found + term
+            stacked = jnp.concatenate(split_parts(field), axis=0)
+            terms = jnp.dot(stacked, COL[...], preferred_element_type=jnp.float32)
+            height = variables * rows
+            found = terms[:height]
+            for part in range(1, PARTS):
+                found = found + terms[part * height : (part + 1) * height]
             for q in range(TILE):
                 hit = sub_r == lax.shift_right_logical(cell_line(chunk * TILE + q), shift_bits)
                 for v in range(variables):
@@ -270,6 +281,7 @@
     p_rel_in = remote(ALLP.at[2], ALLP.at[3 - 2 * odd], ps.at[2], pr.at[1 + odd], inst=sibling)
     p_x.start()
     p_sib.start()
+    forward(0)
     p_x.wait_recv()
     p_rel.start()
     p_sib_in.wait_recv()
@@ -284,9 +296,7 @@
             for u in range(variables):
                 value = ALLP[group, member, u, chunk]
                 for q in range(TILE):
-                    ROUTED[chunk * TILE + q, k * variables + u : k * variables + u + 1, :] = value[
-                        q : q + 1, :
-                    ]
+                    ROUTED[chunk * TILE + q, k, u : u + 1, :] = value[q : q + 1, :]
 
     def a2a(j):
         return remote(
@@ -299,6 +309,7 @@
         a2a(j).start()
 
     ARR[me] = ROUTED[me]
+    forward(1)
     loads[2].wait()
     column_table(target_line, 0)
 
@@ -315,32 +326,27 @@
             column_table(target_line, chunk)
 
         for k in range(per_dev):
-            arrived = [
-                split_parts(ARR[chunk * TILE + p, k * variables : (k + 1) * variables, :])
-                for p in range(TILE)
-            ]
-            hits = [
-                sub_r == lax.shift_right_logical(target_line(chunk * TILE + p), shift_bits)
-                for p in range(TILE)
-            ]
-            for u in range(variables):
-                total_u = None
-                for part in range(3):
-                    spread = jnp.concatenate(
-                        [
-                            jnp.where(
-                                hits[p], arrived[p][part][u : u + 1, :].astype(jnp.float32), 0.0
-                            ).astype(jnp.bfloat16)
-                            for p in range(TILE)
-                        ],
-                        axis=1,
-                    )
-                    term = lax.dot_general(
-                        spread, COL[...], (((1,), (1,)), ((), ())),
-                        preferred_element_type=jnp.float32,
-                    )
-                    total_u = term if total_u is None else total_u + term
-                SP[k, u] = SP[k, u] - total_u
+            for p in range(TILE):
+                hit = sub_r == lax.shift_right_logical(target_line(chunk * TILE + p), shift_bits)
+                parts = split_parts(ARR[chunk * TILE + p, k])
+                for n, part in enumerate(parts):
+                    for u in range(variables):
+                        start = (n * variables + u) * rows
+                        LHS[start : start + rows, p * slots : (p + 1) * slots] = jnp.where(
+                            hit, part[u : u + 1, :].astype(jnp.float32), 0.0
+                        ).astype(jnp.bfloat16)
+            terms = lax.dot_general(
+                LHS[...], COL[...], (((1,), (1,)), ((), ())), preferred_element_type=jnp.float32
+            )
+            height = variables * rows
+            summed = terms[:height]
+            for part in range(1, PARTS):
+                summed = summed + terms[part * height : (part + 1) * height]
+            SP[k] = SP[k] - summed.reshape(variables, rows, width)
+
+    @pl.loop(2, nb - 2)
+    def _(t):
+        forward(t)
 
     for copy in loads[3:]:
         copy.wait()
@@ -378,13 +384,21 @@
         low = pl.ds(row, TILE)
         high = pl.ds(row + 2 * TILE, TILE)
 
-        x_copy(t).wait()
-
-        @pl.when(t + WINDOW < total)
+        @pl.when(t < 2)
+        def _():
+            forward(t + nb - 2)
+
+        @pl.when(t == nb)
+        def _():
+            forward(t)
+
+        @pl.when((t >= nb) & (t + WINDOW < total))
         def _():
             x_copy(t + WINDOW).start()
 
-        relay_copy(t).start()
+        @pl.when((t >= nb) & (t + 1 < total))
+        def _():
+            forward(t + 1)
 
         @pl.when(t == nb)
         def _():
@@ -440,6 +454,10 @@
         def _():
             sib_copy(t + nb).start()
 
+            @pl.when(t < WINDOW)
+            def _():
+                x_copy(t + nb).start()
+
         @pl.when(t == 1)
         def _():
             @pl.when(has_above)
@@ -525,8 +543,9 @@
             pltpu.VMEM((width, TILE * slots), jnp.bfloat16),
             pltpu.VMEM((per_dev, variables, chunks, TILE, slots), f32),
             pltpu.VMEM((4, per_dev, variables, chunks, TILE, slots), f32),
-            pltpu.VMEM((n_space, per_dev * variables, slots), f32),
-            pltpu.VMEM((n_space, per_dev * variables, slots), f32),
+            pltpu.VMEM((n_space, per_dev, variables, slots), f32),
+            pltpu.VMEM((n_space, per_dev, variables, slots), f32),
+            pltpu.VMEM((PARTS * variables * rows, TILE * slots), jnp.bfloat16),
             dma((6,)),
             dma((total,)),
             dma((total,)),

time: 107 us -> 98.2 us (0.918)
  Pallas kernels: 98 us -> 89.4 us
    pallas_call x1, Pallas kernels: 98 us -> 89.4 us  [body(): pl.pallas_call(functools.partial(kernel, n_space), out_shape=(out, out),...]
where the time goes in v1:
time: 98.2 us; the launch traced here: 97.9 us
  Pallas kernels  89.4 us (91%)
  local copies, waits for them, and re-layouts  6.54 us (7%)
  between operations  1.94 us (2%)
    pallas_call x1, Pallas kernels, body(): pl.pallas_call(functools.partial(kernel, n_space), out_shape=(out, out),...  89.4 us
    unnamed x6, local copies, waits for them, and re-layouts  6.54 us

profile of v1, /device:TPU:1, one launch (start us, length us, event | category | flops | bytes accessed | tf_op | source)
XLA Modules:
  0.0 97.9 jit_solution(10347048071349502852)
XLA Ops:
  1.9 1.3 %copy.18.dinv = f32[2,6,6]{2,1,0:T(8,128)} copy(f32[2,6,6]{2,0,1:T(2,128)} %param.22) | data formatting | bytes 576 | tf_op args[7]
  3.2 1.3 %copy.17.blocks = f32[4,6,6]{2,1,0:T(8,128)} copy(f32[4,6,6]{2,0,1:T(4,128)} %param.21) | data formatting | bytes 1152 | tf_op args[6]
  4.5 89.4 %shard_map.158 = (f32[2,6,64,512]{3,2,1,0:T(8,128)}, f32[2,6,64,512]{3,2,1,0:T(8,128)}) custom-call(f32[2,6,64,512]{3,2,1,0:T(8,128)} %a_hbm.1, f32[2,6,64,512]{3,2,1,0:T(8,128)} %s_hbm.1, f32[2,64,512]{2,1,0:T(8,128)} %fs_hbm.1, f32[2,64,512]{2,1,0:T(8,128)} %fp_hbm.1, f32[2,64,512]{2,1,0:T(8,128)} %ds_hbm.1, f32[64,512]{1,0:T(8,128)} %vol_hbm.1, ...), custom_call_target="tpu_custom_call" | custom-call | tf_op jit(solution)/shard_map/pallas_call | solution.py:527
  94.0 0.0 copy-start
  94.0 2.8 %copy.23 = f32[2,6,64,512]{3,2,1,0:T(8,128)} copy(f32[2,6,64,512]{3,2,1,0:T(8,128)} %get-tuple-element.4) | data formatting | bytes 3145728
  96.8 0.0 copy-done
  96.8 1.1 %copy.24 = f32[2,6,64,512]{3,2,1,0:T(8,128)} copy(f32[2,6,64,512]{3,2,1,0:T(8,128)S(1)} %copy-done) | data formatting | bytes 3145728
Async XLA Ops:
  94.0 2.8 %copy-start = (f32[2,6,64,512]{3,2,1,0:T(8,128)S(1)}, f32[2,6,64,512]{3,2,1,0:T(8,128)}, u32[]{:S(2)}) copy-start(f32[2,6,64,512]{3,2,1,0:T(8,128)} %get-tuple-element.5) | copy-start | bytes 4718596
